TPU v7x, 256 devices: a whole 4x4x8 slice. The times are simulated.
256 devices in a mesh: lev: 8 (over z_lo, x), hor: 32 (over z_hi, y, core).
Axes of the slice: x: 4, y: 4, z: 8 (z_hi: 4, z_lo: 2; z = z_hi * 2 + z_lo), core: 2. Of those that a mesh axis runs over, the one named last changes fastest.
Arguments:
- slab_fields: float32 [4, 32, 524288], P(None, 'lev', 'hor'), may hold values from -6 to 6
- sample_index: int32 [32, 1024], P('hor', 'lev'), may hold values from 0 to 2047
- thickness: float32 [32], replicated, may hold values from 0.3 to 3
- level_cuts: int32 [31], replicated, may hold values 0 or 1
Outputs:
- gram: float32 [2176, 2176], P('hor', 'lev')
Inputs may be any that keep to these rules, and one draw needn't show every extreme that they name: sample_index[j, k] indexes a column among the 2048 columns that start at j * 16384 + (k // 128) * 2048.
All inputs are finite; a program needn't handle non-finite values.
Results may differ from a plain program's by a relative error of at most 0.00068.
Values may be sent and summed in bfloat16 or wider, within the bound.
No kernel may reach another device: no remote copies, remote signals or barrier semaphores. Data moves between devices by JAX's collectives and lax.ppermute only.
A program may use at most 128 MiB of HBM per device.

v0:
```python
import jax
import jax.numpy as jnp
from jax import lax
from jax.sharding import PartitionSpec as P


def vertical_filter(values, thickness, level_cuts):
    link = 1.0 - level_cuts.astype(jnp.float32)
    zero_one = jnp.zeros((1,), jnp.float32)
    lower_link = jnp.concatenate([zero_one, link])
    upper_link = jnp.concatenate([link, zero_one])
    lower_weight = jnp.concatenate([zero_one, thickness[:-1]]) * lower_link
    upper_weight = jnp.concatenate([thickness[1:], zero_one]) * upper_link
    zero_row = jnp.zeros_like(values[:, :1, :])
    below = jnp.concatenate([zero_row, values[:, :-1, :]], axis=1)
    above = jnp.concatenate([values[:, 1:, :], zero_row], axis=1)
    numer = (
        2.0 * thickness[None, :, None] * values
        + lower_weight[None, :, None] * below
        + upper_weight[None, :, None] * above
    )
    denom = 2.0 * thickness + lower_weight + upper_weight
    return numer / denom[None, :, None]


def quadratic_features(smooth):
    count = smooth.shape[2]
    later = jnp.concatenate([smooth[2], smooth[3]], axis=0)
    earlier = jnp.concatenate([smooth[0], smooth[1]], axis=0)
    product = (later[:, None, :] * smooth[0][None, :, :]).reshape(-1, count)
    return jnp.concatenate([later, earlier, product], axis=0).astype(jnp.bfloat16)


def on_device(slab_fields, sample_index, thickness, level_cuts):
    samp_count = sample_index.shape[1]
    lev_count = lax.axis_size("lev")
    hor_count = lax.axis_size("hor")
    all_lists = lax.all_gather(sample_index, "lev", axis=1, tiled=True)[0]
    group_cols = slab_fields.shape[2] // lev_count
    offsets = jnp.arange(all_lists.shape[0]) // samp_count * group_cols + all_lists
    chosen = jnp.take(slab_fields, offsets, axis=2)
    picked_cols = lax.all_to_all(chosen, "lev", split_axis=2, concat_axis=1, tiled=True)
    smooth = vertical_filter(picked_cols, thickness, level_cuts)
    feat_count = 4 * smooth.shape[1] + 2 * smooth.shape[1] * smooth.shape[1]
    col_count = feat_count // lev_count
    col_start = lax.axis_index("lev") * col_count
    features_bf = quadratic_features(smooth)
    block_features_bf = lax.all_gather(features_bf, "lev", axis=1, tiled=True)
    chosen_rows = lax.dynamic_slice_in_dim(block_features_bf, col_start, col_count, 0)
    column_block = lax.dot_general(
        block_features_bf, chosen_rows, (((1,), (1,)), ((), ())), preferred_element_type=jnp.float32
    )
    gram_block = lax.psum_scatter(column_block, "hor", scatter_dimension=0, tiled=True)
    count_all = samp_count * lev_count * hor_count
    return gram_block / count_all


def solution(mesh):
    in_specs = (P(None, "lev", "hor"), P("hor", "lev"), P(), P())
    out_specs = P("hor", "lev")
    return jax.shard_map(
        on_device, mesh=mesh, in_specs=in_specs, out_specs=out_specs, check_vma=False
    )
```

profile of v0, /device:TPU:26, one launch (start us, length us, event | category | flops | bytes accessed | tf_op | source)
XLA Modules:
  0.0 281.2 jit_solution(17869697223792710759)
XLA Ops:
  6.5 0.0 copy-start.2
  6.5 21.7 %copy.7 = f32[4,4,16384]{1,0,2:T(4,128)} copy(f32[4,4,16384]{2,1,0:T(4,128)} %param.4) | data formatting | bytes 2097152 | tf_op args[0]
  28.2 0.0 copy-done.2
  28.2 0.0 copy-start.1
  28.2 0.0 copy-start.3
  28.3 16.4 %all_gather.6 = s32[1,1024]{1,0:T(1,128)S(1)} all-gather(s32[1,128]{1,0:T(1,128)S(1)} %copy-done.2), channel_id=1, replica_groups=mesh['lev'=8,'hor'=32] {'lev'}, dimensions={1}, use_global_device_ids=true | all-gather | bytes 4608 | tf_op jit(solution)/shard_map/all_gather | solution.py:38
  44.7 16.8 %gather_fusion = f32[1024,4,4]{2,1,0:T(4,128)} fusion(f32[4,4,16384]{1,0,2:T(4,128)} %copy.7, s32[1024]{0:T(1024)S(1)} %broadcast_clamp_fusion), kind=kCustom, calls=%fused_computation | custom fusion | bytes 135168 | tf_op jit(solution)/shard_map/jit(_take)/gather | solution.py:41
  61.5 5.5 %fusion.18 = f32[1024,4,4]{2,1,0:T(4,128)S(1)} fusion(f32[1024,4,4]{2,1,0:T(4,128)} %gather_fusion, pred[1024]{0:T(1024)(128)(4,1)S(1)} %compare_and_fusion), kind=kLoop, calls=%fused_computation.49 | loop fusion | flops 16384 | bytes 132096
  67.0 3.0 %reshape.135 = f32[8,1,2048]{2,1,0:T(1,128)} reshape(f32[1024,4,4]{2,1,0:T(4,128)S(1)} %fusion.18) | data formatting | bytes 131072
  70.1 6.6 %all-to-all-start = ((f32[8,1,2048]{2,1,0:T(1,128)}), f32[8,1,2048]{2,1,0:T(1,128)S(1)}, u32[]{:S(2)}, u32[]{:S(2)}) async-start(f32[8,1,2048]{2,1,0:T(1,128)} %reshape.135), calls=%async_computation | async-start | bytes 131072 | tf_op jit(solution)/shard_map/all_to_all | solution.py:42
  76.6 0.0 all-gather.2.cloned.1.call-start
  76.6 0.0 copy-done.1
  76.6 0.0 copy-done.3
  76.7 0.1 fusion.17
  76.7 0.1 add_add_fusion
  76.8 4.8 %all-to-all-done = f32[8,1,2048]{2,1,0:T(1,128)S(1)} async-done(((f32[8,1,2048]{2,1,0:T(1,128)}), f32[8,1,2048]{2,1,0:T(1,128)S(1)}, u32[]{:S(2)}, u32[]{:S(2)}) %all-to-all-start) | async-done | bytes 65568 | tf_op jit(solution)/shard_map/all_to_all | solution.py:42
  81.6 0.5 broadcast.122
  82.1 0.8 reduce
  82.9 2.7 reshape.136
  85.6 0.8 copy.8
  86.5 0.1 add_divide_fusion
  86.6 0.1 multiply_convert_fusion
  86.7 0.1 constant_dynamic-update-slice_fusion
  86.8 0.0 copy-start
  86.8 0.8 copy-done
  87.6 0.0 all-gather.2.cloned.1.call-update
  87.7 64.6 %all-gather.2.cloned.1.call-done = bf16[2176,1024]{1,0:T(8,128)(2,1)} async-done(((bf16[2176,128]{1,0:T(8,128)(2,1)}), bf16[2176,1024]{1,0:T(8,128)(2,1)}) %all-gather.2.cloned.1.call-update) | async-done | bytes 4456464 | tf_op jit(solution)/shard_map/all_gather | solution.py:48
  152.2 4.9 %fusion.1 = f32[2176,272]{1,0:T(8,128)S(1)} fusion(bf16[2176,1024]{1,0:T(8,128)(2,1)} %all-gather.2.cloned.1.call-done, s32[]{:T(128)S(6)} %select_n.43), kind=kOutput, calls=%fused_computation.3 | convolution fusion | flops 1212153856 | bytes 7380996 | tf_op jit(solution)/shard_map/dot_general | solution.py:50
  157.1 0.0 copy-start.4
  157.2 75.4 %fusion = f32[80,272]{1,0:T(8,128)S(1)} fusion(f32[2176,272]{1,0:T(8,128)S(1)} %fusion.1), kind=kCustom, calls=%all-reduce-scatter | all-reduce-scatter fusion | flops 696321 | bytes 2455552
  232.6 4.4 %collective-permute-start.3 = (f32[80,272]{1,0:T(8,128)S(1)}, f32[80,272]{1,0:T(8,128)S(1)}, u32[]{:S(2)}, u32[]{:S(2)}) collective-permute-start(f32[80,272]{1,0:T(8,128)S(1)} %fusion), channel_id=1, source_target_pairs={{0,4},{1,5},{2,6},{3,7},{4,8},{5,9},{6,10},{7,11},{8,12},{9,13},{1... | collective-permute-start | bytes 261128
  236.9 8.4 %collective-permute-start.2 = (f32[80,272]{1,0:T(8,128)S(1)}, f32[80,272]{1,0:T(8,128)S(1)}, u32[]{:S(2)}, u32[]{:S(2)}) collective-permute-start(f32[80,272]{1,0:T(8,128)S(1)} %fusion), channel_id=1, source_target_pairs={{0,3},{1,4},{2,5},{3,6},{4,7},{5,8},{6,9},{7,10},{8,11},{9,12},{10... | collective-permute-start | bytes 261128
  245.3 10.9 %collective-permute-start.1 = (f32[80,272]{1,0:T(8,128)S(1)}, f32[80,272]{1,0:T(8,128)S(1)}, u32[]{:S(2)}, u32[]{:S(2)}) collective-permute-start(f32[80,272]{1,0:T(8,128)S(1)} %fusion), channel_id=1, source_target_pairs={{0,2},{1,3},{2,4},{3,5},{4,6},{5,7},{6,8},{7,9},{8,10},{9,11},{10,... | collective-permute-start | bytes 261128
  256.3 8.4 %collective-permute-start = (f32[80,272]{1,0:T(8,128)S(1)}, f32[80,272]{1,0:T(8,128)S(1)}, u32[]{:S(2)}, u32[]{:S(2)}) collective-permute-start(f32[80,272]{1,0:T(8,128)S(1)} %fusion), channel_id=1, source_target_pairs={{0,1},{1,2},{2,3},{3,4},{4,5},{5,6},{6,7},{7,8},{8,9},{9,10},{10,1... | collective-permute-start | bytes 261128
  264.7 1.9 collective-permute-start.4
  266.6 0.0 copy-done.4
  266.6 0.6 dynamic-slice.4
  267.9 4.8 %collective-permute-done.4 = f32[52,272]{1,0:T(8,128)S(1)} collective-permute-done((f32[52,272]{1,0:T(8,128)S(1)}, f32[52,272]{1,0:T(8,128)S(1)}, u32[]{:S(2)}, u32[]{:S(2)}) %collective-permute-start.4) | collective-permute-done | bytes 56608
  272.6 0.0 collective-permute-done.3
  272.6 0.0 collective-permute-done.2
  272.6 0.0 collective-permute-done.1
  272.7 0.0 collective-permute-done
  272.7 1.0 concatenate.50
  273.7 0.7 dynamic-slice_multiply_fusion
  (11 shorter events, 0.1 us)
Async XLA Ops:
  6.5 21.7 %copy-start.2 = (s32[1,128]{1,0:T(1,128)S(1)}, s32[1,128]{1,0:T(1,128)}, u32[]{:S(2)}) copy-start(s32[1,128]{1,0:T(1,128)} %param.5) | copy-start | bytes 1540
  28.2 48.4 %copy-start.1 = (f32[32]{0:T(128)S(1)}, f32[32]{0:T(128)}, u32[]{:S(2)}) copy-start(f32[32]{0:T(128)} %param.6) | copy-start | bytes 388
  28.2 48.4 %copy-start.3 = (s32[31]{0:T(128)S(1)}, s32[31]{0:T(128)}, u32[]{:S(2)}) copy-start(s32[31]{0:T(128)} %param.7) | copy-start | bytes 376
  70.1 11.5 %all-to-all-start = ((f32[8,1,2048]{2,1,0:T(1,128)}), f32[8,1,2048]{2,1,0:T(1,128)S(1)}, u32[]{:S(2)}, u32[]{:S(2)}) async-start(f32[8,1,2048]{2,1,0:T(1,128)} %reshape.135), calls=%async_computation | async-start | bytes 131072 | tf_op jit(solution)/shard_map/all_to_all | solution.py:42
  76.6 75.6 %all-gather.2.cloned.1.call-start = ((), (), s32[]{:S(2)}) async-start(), calls=%async_computation.1 | async-start | bytes 5013504 | tf_op jit(solution)/shard_map/all_gather | solution.py:48
  86.8 0.8 copy-start
  157.1 109.5 %copy-start.4 = (u32[256]{0:T(256)S(1)}, u32[256]{0:T(256)}, u32[]{:S(2)}) copy-start(u32[256]{0:T(256)} %constant.76) | copy-start | bytes 3076
  232.6 40.1 %collective-permute-start.3 = (f32[80,272]{1,0:T(8,128)S(1)}, f32[80,272]{1,0:T(8,128)S(1)}, u32[]{:S(2)}, u32[]{:S(2)}) collective-permute-start(f32[80,272]{1,0:T(8,128)S(1)} %fusion), channel_id=1, source_target_pairs={{0,4},{1,5},{2,6},{3,7},{4,8},{5,9},{6,10},{7,11},{8,12},{9,13},{1... | collective-permute-start | bytes 261128
  236.9 35.7 %collective-permute-start.2 = (f32[80,272]{1,0:T(8,128)S(1)}, f32[80,272]{1,0:T(8,128)S(1)}, u32[]{:S(2)}, u32[]{:S(2)}) collective-permute-start(f32[80,272]{1,0:T(8,128)S(1)} %fusion), channel_id=1, source_target_pairs={{0,3},{1,4},{2,5},{3,6},{4,7},{5,8},{6,9},{7,10},{8,11},{9,12},{10... | collective-permute-start | bytes 261128
  245.3 27.3 %collective-permute-start.1 = (f32[80,272]{1,0:T(8,128)S(1)}, f32[80,272]{1,0:T(8,128)S(1)}, u32[]{:S(2)}, u32[]{:S(2)}) collective-permute-start(f32[80,272]{1,0:T(8,128)S(1)} %fusion), channel_id=1, source_target_pairs={{0,2},{1,3},{2,4},{3,5},{4,6},{5,7},{6,8},{7,9},{8,10},{9,11},{10,... | collective-permute-start | bytes 261128
  256.3 16.4 %collective-permute-start = (f32[80,272]{1,0:T(8,128)S(1)}, f32[80,272]{1,0:T(8,128)S(1)}, u32[]{:S(2)}, u32[]{:S(2)}) collective-permute-start(f32[80,272]{1,0:T(8,128)S(1)} %fusion), channel_id=1, source_target_pairs={{0,1},{1,2},{2,3},{3,4},{4,5},{5,6},{6,7},{7,8},{8,9},{9,10},{10,1... | collective-permute-start | bytes 261128
  264.7 7.9 %collective-permute-start.4 = (f32[52,272]{1,0:T(8,128)S(1)}, f32[52,272]{1,0:T(8,128)S(1)}, u32[]{:S(2)}, u32[]{:S(2)}) collective-permute-start(f32[52,272]{1,0:T(8,128)S(1)} %slice.42), channel_id=1, source_target_pairs={{0,5},{1,6},{2,7},{3,8},{4,9},{5,10},{6,11},{7,12},{8,13},{9,14},{... | collective-permute-start | bytes 169736
Sparse Core Ops, SparseCore 0:
  87.8 64.4 all-gather.1
where the time goes:
time: 284 us; the launch traced here: 281 us
  blocking collectives  91.9 us (32%)
  waiting for transfers between devices  74.1 us (26%)
  local copies, waits for them, and re-layouts  48.2 us (17%)
  starting transfers between devices  40.6 us (14%)
  between operations  14.3 us (5%)
  other arithmetic  7.31 us (3%)
  matrix products  4.9 us (2%)
    unnamed x1, blocking collectives  75.4 us
    all_gather x1, waiting for transfers between devices, on_device(): block_features_bf = lax.all_gather(features_bf, 'lev', axis=1, tiled=True)  64.6 us
    unnamed x5, starting transfers between devices  34 us
    unnamed x20, local copies, waits for them, and re-layouts  30 us
    gather x1, local copies, waits for them, and re-layouts, on_device(): chosen = jnp.take(slab_fields, offsets, axis=2)  16.8 us
    all_gather x1, blocking collectives, on_device(): all_lists = lax.all_gather(sample_index, 'lev', axis=1, tiled=True)[0]  16.4 us
    all_to_all x1, starting transfers between devices, on_device(): lax.all_to_all(chosen, 'lev', split_axis=2, concat_axis=1, tiled=True)  6.56 us
  transfers between devices with their start and end apart: 7, of which 3 were waited for; matrix products, arithmetic and copies ran while one was open for 0% of the time, Pallas kernels for 0%

commit v1 on v0

--- a/solution.py
+++ b/solution.py
@@ -45,7 +45,10 @@
     col_count = feat_count // lev_count
     col_start = lax.axis_index("lev") * col_count
     features_bf = quadratic_features(smooth)
-    block_features_bf = lax.all_gather(features_bf, "lev", axis=1, tiled=True)
+    size = lax.axis_size("lev")
+    blocks = jnp.stack([features_bf for _ in range(size)])
+    blocks = lax.all_to_all(blocks, "lev", split_axis=0, concat_axis=0)
+    block_features_bf = jnp.concatenate(blocks, axis=1)
     chosen_rows = lax.dynamic_slice_in_dim(block_features_bf, col_start, col_count, 0)
     column_block = lax.dot_general(
         block_features_bf, chosen_rows, (((1,), (1,)), ((), ())), preferred_element_type=jnp.float32

time: 284 us -> 259 us (0.912)
  the two profiles are of different devices: /device:TPU:26 before, /device:TPU:30 now
where the time goes in v1:
time: 259 us; the launch traced here: 257 us
  blocking collectives  91.8 us (35%)
  waiting for transfers between devices  54 us (21%)
  local copies, waits for them, and re-layouts  50.3 us (19%)
  starting transfers between devices  47.1 us (18%)
  other arithmetic  7.31 us (3%)
  matrix products  5.15 us (2%)
    unnamed x1, blocking collectives  76.9 us
    all_to_all x1, waiting for transfers between devices, on_device(): blocks = lax.all_to_all(blocks, 'lev', split_axis=0, concat_axis=0)  45.1 us
    unnamed x5, starting transfers between devices  32.5 us
    unnamed x18, local copies, waits for them, and re-layouts  29.1 us
    gather x1, local copies, waits for them, and re-layouts, on_device(): chosen = jnp.take(slab_fields, offsets, axis=2)  16.8 us
    all_gather x1, blocking collectives, on_device(): all_lists = lax.all_gather(sample_index, 'lev', axis=1, tiled=True)[0]  14.9 us
    all_to_all x1, starting transfers between devices, on_device(): lax.all_to_all(chosen, 'lev', split_axis=2, concat_axis=1, tiled=True)  8.08 us
    all_to_all x1, starting transfers between devices, on_device(): blocks = lax.all_to_all(blocks, 'lev', split_axis=0, concat_axis=0)  6.54 us
  transfers between devices with their start and end apart: 7, of which 3 were waited for; matrix products, arithmetic and copies ran while one was open for 0% of the time, Pallas kernels for 0%

profile of v1, /device:TPU:30, one launch (start us, length us, event | category | flops | bytes accessed | tf_op | source)
XLA Modules:
  0.0 256.6 jit_solution(7957375144239462190)
XLA Ops:
  0.0 0.0 copy-start.1
  0.0 21.7 %copy.16 = f32[4,4,16384]{1,0,2:T(4,128)} copy(f32[4,4,16384]{2,1,0:T(4,128)} %param.4) | data formatting | bytes 2097152 | tf_op args[0]
  21.7 0.0 copy-done.1
  21.7 0.0 copy-start
  21.7 0.0 copy-start.2
  21.7 14.9 %all_gather.3 = s32[1,1024]{1,0:T(1,128)S(1)} all-gather(s32[1,128]{1,0:T(1,128)S(1)} %copy-done.1), channel_id=1, replica_groups=mesh['lev'=8,'hor'=32] {'lev'}, dimensions={1}, use_global_device_ids=true | all-gather | bytes 4608 | tf_op jit(solution)/shard_map/all_gather | solution.py:38
  36.6 16.8 %gather_fusion = f32[1024,4,4]{2,1,0:T(4,128)} fusion(f32[4,4,16384]{1,0,2:T(4,128)} %copy.16, s32[1024]{0:T(1024)S(1)} %broadcast_clamp_fusion), kind=kCustom, calls=%fused_computation | custom fusion | bytes 135168 | tf_op jit(solution)/shard_map/jit(_take)/gather | solution.py:41
  53.4 5.5 %fusion.18 = f32[1024,4,4]{2,1,0:T(4,128)S(1)} fusion(f32[1024,4,4]{2,1,0:T(4,128)} %gather_fusion, pred[1024]{0:T(1024)(128)(4,1)S(1)} %compare_and_fusion), kind=kLoop, calls=%fused_computation.49 | loop fusion | flops 16384 | bytes 132096
  58.9 3.0 %reshape.164 = f32[8,1,2048]{2,1,0:T(1,128)} reshape(f32[1024,4,4]{2,1,0:T(4,128)S(1)} %fusion.18) | data formatting | bytes 131072
  61.9 8.1 %all-to-all-start = ((f32[8,1,2048]{2,1,0:T(1,128)}), f32[8,1,2048]{2,1,0:T(1,128)S(1)}, u32[]{:S(2)}, u32[]{:S(2)}) async-start(f32[8,1,2048]{2,1,0:T(1,128)} %reshape.164), calls=%async_computation | async-start | bytes 131072 | tf_op jit(solution)/shard_map/all_to_all | solution.py:42
  70.0 0.0 copy-done
  70.0 0.0 copy-done.2
  70.0 0.1 fusion.17
  70.1 0.1 add_add_fusion
  70.2 4.1 %all-to-all-done = f32[8,1,2048]{2,1,0:T(1,128)S(1)} async-done(((f32[8,1,2048]{2,1,0:T(1,128)}), f32[8,1,2048]{2,1,0:T(1,128)S(1)}, u32[]{:S(2)}, u32[]{:S(2)}) %all-to-all-start) | async-done | bytes 65568 | tf_op jit(solution)/shard_map/all_to_all | solution.py:42
  74.3 0.5 broadcast.123
  74.8 0.8 reduce
  75.6 2.7 %reshape.165 = f32[1024,4,4]{2,1,0:T(4,128)S(1)} reshape(f32[8,2048]{1,0:T(8,128)S(1)} %reduce) | data formatting | bytes 131072
  78.4 0.8 copy.17
  79.2 0.1 add_divide_fusion
  79.4 0.1 multiply_convert_fusion
  79.5 0.1 constant_dynamic-update-slice_fusion
  79.6 0.3 copy.18
  79.9 2.7 %stack.2 = bf16[8,2176,128]{1,2,0:T(8,128)(2,1)} broadcast(bf16[2176,128]{0,1:T(8,128)(2,1)S(1)} %copy.18), dimensions={1,2} | broadcast | bytes 5013504 | tf_op jit(solution)/shard_map/stack | solution.py:49
  82.5 6.5 %all-to-all-start.1 = ((bf16[8,2176,128]{1,2,0:T(8,128)(2,1)}), bf16[8,2176,128]{1,2,0:T(8,128)(2,1)}, u32[]{:S(2)}, u32[]{:S(2)}) async-start(bf16[8,2176,128]{1,2,0:T(8,128)(2,1)} %stack.2), calls=%async_computation.1 | async-start | bytes 8912896 | tf_op jit(solution)/shard_map/all_to_all | solution.py:50
  89.1 45.1 %all-to-all-done.1 = bf16[8,2176,128]{1,2,0:T(8,128)(2,1)} async-done(((bf16[8,2176,128]{1,2,0:T(8,128)(2,1)}), bf16[8,2176,128]{1,2,0:T(8,128)(2,1)}, u32[]{:S(2)}, u32[]{:S(2)}) %all-to-all-start.1) | async-done | bytes 4456480 | tf_op jit(solution)/shard_map/all_to_all | solution.py:50
  134.2 5.1 %fusion.1 = f32[2176,272]{1,0:T(8,128)S(1)} fusion(bf16[2176,1024]{0,1:T(8,128)(2,1)} %bitcast.14, s32[]{:T(128)S(6)} %select_n.43), kind=kOutput, calls=%fused_computation.3 | convolution fusion | flops 1212153856 | bytes 7610372 | tf_op jit(solution)/shard_map/dot_general | solution.py:53
  139.3 0.0 copy-start.3
  139.4 76.9 %fusion = f32[80,272]{1,0:T(8,128)S(1)} fusion(f32[2176,272]{1,0:T(8,128)S(1)} %fusion.1), kind=kCustom, calls=%all-reduce-scatter | all-reduce-scatter fusion | flops 696321 | bytes 2455552
  216.3 7.7 %collective-permute-start.3 = (f32[80,272]{1,0:T(8,128)S(1)}, f32[80,272]{1,0:T(8,128)S(1)}, u32[]{:S(2)}, u32[]{:S(2)}) collective-permute-start(f32[80,272]{1,0:T(8,128)S(1)} %fusion), channel_id=1, source_target_pairs={{0,4},{1,5},{2,6},{3,7},{4,8},{5,9},{6,10},{7,11},{8,12},{9,13},{1... | collective-permute-start | bytes 261128
  224.0 3.9 %collective-permute-start.2 = (f32[80,272]{1,0:T(8,128)S(1)}, f32[80,272]{1,0:T(8,128)S(1)}, u32[]{:S(2)}, u32[]{:S(2)}) collective-permute-start(f32[80,272]{1,0:T(8,128)S(1)} %fusion), channel_id=1, source_target_pairs={{0,3},{1,4},{2,5},{3,6},{4,7},{5,8},{6,9},{7,10},{8,11},{9,12},{10... | collective-permute-start | bytes 261128
  227.9 10.7 %collective-permute-start.1 = (f32[80,272]{1,0:T(8,128)S(1)}, f32[80,272]{1,0:T(8,128)S(1)}, u32[]{:S(2)}, u32[]{:S(2)}) collective-permute-start(f32[80,272]{1,0:T(8,128)S(1)} %fusion), channel_id=1, source_target_pairs={{0,2},{1,3},{2,4},{3,5},{4,6},{5,7},{6,8},{7,9},{8,10},{9,11},{10,... | collective-permute-start | bytes 261128
  238.6 8.3 %collective-permute-start = (f32[80,272]{1,0:T(8,128)S(1)}, f32[80,272]{1,0:T(8,128)S(1)}, u32[]{:S(2)}, u32[]{:S(2)}) collective-permute-start(f32[80,272]{1,0:T(8,128)S(1)} %fusion), channel_id=1, source_target_pairs={{0,1},{1,2},{2,3},{3,4},{4,5},{5,6},{6,7},{7,8},{8,9},{9,10},{10,1... | collective-permute-start | bytes 261128
  246.9 1.9 collective-permute-start.4
  248.9 0.0 copy-done.3
  248.9 0.6 dynamic-slice.4
  250.1 4.8 %collective-permute-done.4 = f32[52,272]{1,0:T(8,128)S(1)} collective-permute-done((f32[52,272]{1,0:T(8,128)S(1)}, f32[52,272]{1,0:T(8,128)S(1)}, u32[]{:S(2)}, u32[]{:S(2)}) %collective-permute-start.4) | collective-permute-done | bytes 56608
  254.9 0.0 collective-permute-done.3
  254.9 0.0 collective-permute-done.2
  254.9 0.0 collective-permute-done.1
  254.9 0.0 collective-permute-done
  254.9 1.0 concatenate.64
  255.9 0.7 dynamic-slice_multiply_fusion
  (11 shorter events, 0.1 us)
Async XLA Ops:
  0.0 21.7 %copy-start.1 = (s32[1,128]{1,0:T(1,128)S(1)}, s32[1,128]{1,0:T(1,128)}, u32[]{:S(2)}) copy-start(s32[1,128]{1,0:T(1,128)} %param.5) | copy-start | bytes 1540
  21.7 48.3 %copy-start = (f32[32]{0:T(128)S(1)}, f32[32]{0:T(128)}, u32[]{:S(2)}) copy-start(f32[32]{0:T(128)} %param.6) | copy-start | bytes 388
  21.7 48.3 %copy-start.2 = (s32[31]{0:T(128)S(1)}, s32[31]{0:T(128)}, u32[]{:S(2)}) copy-start(s32[31]{0:T(128)} %param.7) | copy-start | bytes 376
  61.9 12.4 %all-to-all-start = ((f32[8,1,2048]{2,1,0:T(1,128)}), f32[8,1,2048]{2,1,0:T(1,128)S(1)}, u32[]{:S(2)}, u32[]{:S(2)}) async-start(f32[8,1,2048]{2,1,0:T(1,128)} %reshape.164), calls=%async_computation | async-start | bytes 131072 | tf_op jit(solution)/shard_map/all_to_all | solution.py:42
  82.5 51.7 %all-to-all-start.1 = ((bf16[8,2176,128]{1,2,0:T(8,128)(2,1)}), bf16[8,2176,128]{1,2,0:T(8,128)(2,1)}, u32[]{:S(2)}, u32[]{:S(2)}) async-start(bf16[8,2176,128]{1,2,0:T(8,128)(2,1)} %stack.2), calls=%async_computation.1 | async-start | bytes 8912896 | tf_op jit(solution)/shard_map/all_to_all | solution.py:50
  139.3 109.5 %copy-start.3 = (u32[256]{0:T(256)S(1)}, u32[256]{0:T(256)}, u32[]{:S(2)}) copy-start(u32[256]{0:T(256)} %constant.76) | copy-start | bytes 3076
  216.3 38.6 %collective-permute-start.3 = (f32[80,272]{1,0:T(8,128)S(1)}, f32[80,272]{1,0:T(8,128)S(1)}, u32[]{:S(2)}, u32[]{:S(2)}) collective-permute-start(f32[80,272]{1,0:T(8,128)S(1)} %fusion), channel_id=1, source_target_pairs={{0,4},{1,5},{2,6},{3,7},{4,8},{5,9},{6,10},{7,11},{8,12},{9,13},{1... | collective-permute-start | bytes 261128
  224.0 30.9 %collective-permute-start.2 = (f32[80,272]{1,0:T(8,128)S(1)}, f32[80,272]{1,0:T(8,128)S(1)}, u32[]{:S(2)}, u32[]{:S(2)}) collective-permute-start(f32[80,272]{1,0:T(8,128)S(1)} %fusion), channel_id=1, source_target_pairs={{0,3},{1,4},{2,5},{3,6},{4,7},{5,8},{6,9},{7,10},{8,11},{9,12},{10... | collective-permute-start | bytes 261128
  227.9 27.0 %collective-permute-start.1 = (f32[80,272]{1,0:T(8,128)S(1)}, f32[80,272]{1,0:T(8,128)S(1)}, u32[]{:S(2)}, u32[]{:S(2)}) collective-permute-start(f32[80,272]{1,0:T(8,128)S(1)} %fusion), channel_id=1, source_target_pairs={{0,2},{1,3},{2,4},{3,5},{4,6},{5,7},{6,8},{7,9},{8,10},{9,11},{10,... | collective-permute-start | bytes 261128
  238.6 16.3 %collective-permute-start = (f32[80,272]{1,0:T(8,128)S(1)}, f32[80,272]{1,0:T(8,128)S(1)}, u32[]{:S(2)}, u32[]{:S(2)}) collective-permute-start(f32[80,272]{1,0:T(8,128)S(1)} %fusion), channel_id=1, source_target_pairs={{0,1},{1,2},{2,3},{3,4},{4,5},{5,6},{6,7},{7,8},{8,9},{9,10},{10,1... | collective-permute-start | bytes 261128
  246.9 7.9 %collective-permute-start.4 = (f32[52,272]{1,0:T(8,128)S(1)}, f32[52,272]{1,0:T(8,128)S(1)}, u32[]{:S(2)}, u32[]{:S(2)}) collective-permute-start(f32[52,272]{1,0:T(8,128)S(1)} %slice.42), channel_id=1, source_target_pairs={{0,5},{1,6},{2,7},{3,8},{4,9},{5,10},{6,11},{7,12},{8,13},{9,14},{... | collective-permute-start | bytes 169736
